TPU v7x, 32 devices: a whole 2x2x4 slice. The times are simulated.
32 devices in a mesh: group: 2 (over y), expert: 16 (over z, x, core).
Axes of the slice: x: 2, y: 2, z: 4, core: 2. Of those that a mesh axis runs over, the one named last changes fastest.
Arguments:
- tokens: bfloat16 [256, 7168], P(('group', 'expert')), parts along dimension 0, may hold values from -6 to 6
- expert_ids: int32 [256, 8], P(('group', 'expert')), parts along dimension 0, may hold values from 0 to 15, all different within a row; in each aligned block of 8 rows (0 to 7, 8 to 15, ...) at most 5 rows name the same one
- gate_probs: float32 [256, 8], P(('group', 'expert')), parts along dimension 0, may hold values from 0.05 to 0.6
- gate_proj: bfloat16 [7168, 32768], P(None, 'expert'), may hold values from -0.0625 to 0.0625
- up_proj: bfloat16 [7168, 32768], P(None, 'expert'), may hold values from -0.0625 to 0.0625
- down_proj: bfloat16 [32768, 7168], P('expert'), may hold values from -0.125 to 0.125
Outputs:
- mixed: bfloat16 [256, 7168], P(('group', 'expert')), parts along dimension 0
There are 2 independent parts, one for each index of `group`. A program takes and returns all parts, laid end to end along the dimension named above; an argument that names none is the same for every part. Nothing has to cross between parts.
Inputs may be any that keep to these rules, and one draw needn't show every extreme that they name: `expert_ids`: each row names 8 different experts. Among the 8 tokens of one device (aligned blocks of 8 rows) no expert is named by more than 5 tokens, a bound that some blocks reach.
All inputs are finite; a program needn't handle non-finite values.
Results may differ from a plain program's by a relative error of at most 0.0051.
Values may be sent and summed in bfloat16 or wider, within the bound.
No kernel may reach another device: no remote copies, remote signals or barrier semaphores. Data moves between devices by JAX's collectives and lax.ppermute only.
A program may use at most 192 MiB of HBM per device.

v0:
```python
import jax
import jax.numpy as jnp
from jax import lax
from jax.sharding import PartitionSpec as P

FF = 2048
EXPERTS = 16
CAP = 5


def shards(tokens, expert_ids, gate_probs, gate_proj, up_proj, down_proj):
    hid_count = gate_proj.shape[1]
    splits = FF // hid_count
    tok_count, model_width = tokens.shape
    devices = lax.axis_size("expert")
    picks = expert_ids[:, :, None] == jnp.arange(EXPERTS, dtype=jnp.int32)[None, None, :]
    chosen = jnp.sum(picks.astype(jnp.int32), axis=1)
    weight_te = jnp.sum(jnp.where(picks, gate_probs[:, :, None], 0.0), axis=1)
    slot_of = jnp.cumsum(chosen, axis=0) - 1
    placed = (chosen[:, :, None] == 1) & (
        slot_of[:, :, None] == jnp.arange(CAP, dtype=jnp.int32)[None, None, :]
    )
    picked = placed.astype(jnp.bfloat16)
    combine_w = jnp.where(placed, weight_te[:, :, None], 0.0)
    packed = jnp.einsum("tec,td->ecd", picked, tokens, preferred_element_type=jnp.float32).astype(
        jnp.bfloat16
    )
    outgoing = jnp.broadcast_to(packed[:, None], (EXPERTS, splits, CAP, model_width)).reshape(
        devices, CAP, model_width
    )
    blocks = lax.all_to_all(outgoing, "expert", split_axis=0, concat_axis=0, tiled=True)
    flat_rows = blocks.reshape(-1, model_width)
    gate_val = jnp.dot(flat_rows, gate_proj, preferred_element_type=jnp.float32)
    up_val = jnp.dot(flat_rows, up_proj, preferred_element_type=jnp.float32)
    hidden = (jax.nn.silu(gate_val) * up_val).astype(jnp.bfloat16)
    result = jnp.dot(hidden, down_proj, preferred_element_type=jnp.float32)
    partial_value = result.reshape(blocks.shape[0], blocks.shape[1], model_width)
    returned = lax.all_to_all(partial_value, "expert", split_axis=0, concat_axis=0, tiled=True)
    returned = returned.reshape(EXPERTS, splits, CAP, model_width)
    combined = jnp.einsum("tec,escd->td", combine_w, returned, precision=lax.Precision.HIGHEST)
    return combined.astype(jnp.bfloat16)


def solution(mesh):
    placed = (
        P(("group", "expert"), None),
        P(("group", "expert"), None),
        P(("group", "expert"), None),
        P(None, "expert"),
        P(None, "expert"),
        P("expert", None),
    )
    return jax.shard_map(
        shards, mesh=mesh, in_specs=placed, out_specs=P(("group", "expert"), None), check_vma=False
    )
```

profile of v0, /device:TPU:15, one launch (start us, length us, event | category | flops | bytes accessed | tf_op | source)
XLA Modules:
  0.0 180.2 jit_solution(9811228272586178524)
XLA Ops:
  0.0 0.0 copy-start
  0.0 0.8 convert_reduce_fusion
  0.8 0.0 copy-start.5
  0.9 0.0 copy-start.2
  0.9 0.6 copy-done.2
  1.5 0.0 copy-done
  1.5 0.5 convolution_convert_fusion
  2.0 0.7 copy.12
  2.6 0.0 copy-done.5
  2.6 48.0 %all_to_all.10 = bf16[16,5,7168]{2,1,0:T(8,128)(2,1)S(1)} all-to-all(bf16[16,5,7168]{2,1,0:T(8,128)(2,1)S(1)} %copy.12), channel_id=1, replica_groups=mesh['group'=2,'expert'=16] {'expert'}, dimensions={0} | all-to-all | bytes 2293760 | tf_op jit(solution)/shard_map/all_to_all | solution.py:31
  50.7 0.6 reshape.23
  51.2 12.9 %fusion.23 = f32[80,2048]{1,0:T(8,128)} fusion(bf16[80,7168]{1,0:T(8,128)(2,1)S(1)} %reshape.23, bf16[7168,2048]{1,0:T(8,128)(2,1)} %param.9), kind=kOutput, calls=%fused_computation.30 | convolution fusion | flops 2348810240 | bytes 31162368 | tf_op jit(solution)/shard_map/dot_general | solution.py:33
  64.1 21.0 %fusion.2 = f32[80,7168]{1,0:T(8,128)S(1)} fusion(bf16[2048,7168]{1,0:T(8,128)(2,1)} %param.11, bf16[80,7168]{1,0:T(8,128)(2,1)S(1)} %reshape.23, bf16[7168,2048]{1,0:T(8,128)(2,1)} %param.10, f32[80,2048]{1,0:T(8,128)} %fusion.23), kind=kOutput, calls=%fused_computation.5 | convolution fusion | flops 4698603520 | bytes 62816256 | tf_op jit(solution)/shard_map/dot_general | solution.py:36
  85.1 0.0 copy-start.1
  85.1 2.0 %reshape.24 = f32[16,5,7168]{2,1,0:T(8,128)} reshape(f32[80,7168]{1,0:T(8,128)S(1)} %fusion.2) | data formatting | bytes 4587520 | tf_op jit(solution)/shard_map/reshape | solution.py:37
  87.2 0.0 copy-start.4
  87.2 0.0 copy-start.7
  87.2 0.0 copy-start.3
  87.2 0.0 copy-start.6
  87.2 5.6 %all-to-all-start.1 = ((f32[16,5,7168]{2,1,0:T(8,128)}), f32[16,5,7168]{2,1,0:T(8,128)}, u32[]{:S(2)}, u32[]{:S(2)}) async-start(f32[16,5,7168]{2,1,0:T(8,128)} %reshape.24), calls=%async_computation.1 | async-start | bytes 7340032 | tf_op jit(solution)/shard_map/all_to_all | solution.py:38
  92.8 0.0 copy-done.4
  92.8 0.0 copy-done.7
  92.8 0.1 select_reduce_fusion
  92.9 81.1 %all-to-all-done.1 = f32[16,5,7168]{2,1,0:T(8,128)} async-done(((f32[16,5,7168]{2,1,0:T(8,128)}), f32[16,5,7168]{2,1,0:T(8,128)}, u32[]{:S(2)}, u32[]{:S(2)}) %all-to-all-start.1) | async-done | bytes 2293792 | tf_op jit(solution)/shard_map/all_to_all | solution.py:38
  174.0 0.0 copy-done.3
  174.0 0.0 copy-done.6
  174.0 6.2 %fusion = bf16[8,7168]{1,0:T(8,128)(2,1)} fusion(f32[16,5,7168]{2,1,0:T(8,128)} %all-to-all-done.1, f32[8,16]{1,0:T(8,128)S(1)} %select_reduce_fusion, s32[8,16]{1,0:T(8,128)S(1)} %copy-done.3, pred[8,16]{1,0:T(8,128)(4,1)S(1)} %copy-done.6), kind=kOutput, calls=%fused_computation.2 | convolution fusion | flops 55109504 | bytes 2409600 | tf_op jit(solution)/shard_map/tec,escd->td/dot_general | solution.py:40
  180.2 0.0 copy-done.1
  (3 shorter events, 0.0 us)
Async XLA Ops:
  0.0 1.5 copy-start
  0.8 1.8 copy-start.5
  0.9 0.6 copy-start.2
  85.1 95.1 %copy-start.1 = (bf16[8,7168]{1,0:T(8,128)(2,1)S(1)}, bf16[8,7168]{1,0:T(8,128)(2,1)}, u32[]{:S(2)}) copy-start(bf16[8,7168]{1,0:T(8,128)(2,1)} %param.6) | copy-start | bytes 344068
  87.2 5.6 %copy-start.4 = (s32[8,8]{1,0:T(8,128)S(1)}, s32[8,8]{1,0:T(8,128)}, u32[]{:S(2)}) copy-start(s32[8,8]{1,0:T(8,128)} %param.7) | copy-start | bytes 772
  87.2 5.6 %copy-start.7 = (f32[8,8]{1,0:T(8,128)S(1)}, f32[8,8]{1,0:T(8,128)}, u32[]{:S(2)}) copy-start(f32[8,8]{1,0:T(8,128)} %param.8) | copy-start | bytes 772
  87.2 86.8 %copy-start.3 = (s32[8,16]{1,0:T(8,128)S(1)}, s32[8,16]{1,0:T(8,128)}, u32[]{:S(2)}) copy-start(s32[8,16]{1,0:T(8,128)} %copy-done.2) | copy-start | bytes 1540
  87.2 86.8 %copy-start.6 = (pred[8,16]{1,0:T(8,128)(4,1)S(1)}, pred[8,16]{1,0:T(8,128)(4,1)}, u32[]{:S(2)}) copy-start(pred[8,16]{1,0:T(8,128)(4,1)} %copy-done.5) | copy-start | bytes 388
  87.2 86.8 %all-to-all-start.1 = ((f32[16,5,7168]{2,1,0:T(8,128)}), f32[16,5,7168]{2,1,0:T(8,128)}, u32[]{:S(2)}, u32[]{:S(2)}) async-start(f32[16,5,7168]{2,1,0:T(8,128)} %reshape.24), calls=%async_computation.1 | async-start | bytes 7340032 | tf_op jit(solution)/shard_map/all_to_all | solution.py:38
where the time goes:
time: 180 us
  waiting for transfers between devices  81.1 us (45%)
  blocking collectives  48 us (27%)
  matrix products  40.5 us (22%)
  starting transfers between devices  5.58 us (3%)
  local copies, waits for them, and re-layouts  3.86 us (2%)
    all_to_all x1, waiting for transfers between devices, shards(): lax.all_to_all(partial_value, 'expert', split_axis=0, concat_axis=0, tile...  81.1 us
    all_to_all x1, blocking collectives, shards(): lax.all_to_all(outgoing, 'expert', split_axis=0, concat_axis=0, tiled=True)  48 us
    dot_general x1, matrix products, shards(): result = jnp.dot(hidden, down_proj, preferred_element_type=jnp.float32)  21 us
    dot_general x1, matrix products, shards(): gate_val = jnp.dot(flat_rows, gate_proj, preferred_element_type=jnp.float32)  12.9 us
    dot_general x1, matrix products, shards(): jnp.einsum('tec,escd->td', combine_w, returned, precision=lax.Precision.H...  6.16 us
    all_to_all x1, starting transfers between devices, shards(): lax.all_to_all(partial_value, 'expert', split_axis=0, concat_axis=0, tile...  5.58 us
  transfers between devices with their start and end apart: 1, of which 1 were waited for; matrix products, arithmetic and copies ran while one was open for 0% of the time, Pallas kernels for 0%

commit v1 on v0

--- a/solution.py
+++ b/solution.py
@@ -6,6 +6,22 @@
 FF = 2048
 EXPERTS = 16
 CAP = 5
+
+
+def exchange_in_pairs(shard, axis, split, join):
+    ways, here = (lax.axis_size(axis), lax.axis_index(axis))
+    width = shard.shape[split] // ways
+    dims = list(shard.shape)
+    dims[split] = width
+    height = dims[join]
+    dims[join] = height * ways
+    full = jnp.zeros(dims, shard.dtype)
+    for mask in range(ways):
+        part = lax.dynamic_slice_in_dim(shard, (here ^ mask) * width, width, axis=split)
+        if mask:
+            part = lax.ppermute(part, axis, [(d, d ^ mask) for d in range(ways)])
+        full = lax.dynamic_update_slice_in_dim(full, part, (here ^ mask) * height, axis=join)
+    return full
 
 
 def shards(tokens, expert_ids, gate_probs, gate_proj, up_proj, down_proj):
@@ -28,7 +44,7 @@
     outgoing = jnp.broadcast_to(packed[:, None], (EXPERTS, splits, CAP, model_width)).reshape(
         devices, CAP, model_width
     )
-    blocks = lax.all_to_all(outgoing, "expert", split_axis=0, concat_axis=0, tiled=True)
+    blocks = exchange_in_pairs(outgoing, "expert", 0, 0)
     flat_rows = blocks.reshape(-1, model_width)
     gate_val = jnp.dot(flat_rows, gate_proj, preferred_element_type=jnp.float32)
     up_val = jnp.dot(flat_rows, up_proj, preferred_element_type=jnp.float32)

time: 180 us -> 196 us (1.089)
  blocking collectives: 48 us -> 0 us
  waiting for transfers between devices: 81.1 us -> 124 us
  starting transfers between devices: 5.58 us -> 24 us
  local copies, waits for them, and re-layouts: 3.86 us -> 6.16 us
    all_to_all x1 -> x0, blocking collectives: 48 us -> none  [shards(): lax.all_to_all(outgoing, 'expert', split_axis=0, concat_axis=0, tiled=True)]
    ppermute x0 -> x15, waiting for transfers between devices: none -> 42.7 us  [exchange_in_pairs(): part = lax.ppermute(part, axis, [(d, d ^ mask) for d in range(ways)])]
    ppermute x0 -> x15, starting transfers between devices: none -> 17.7 us  [exchange_in_pairs(): part = lax.ppermute(part, axis, [(d, d ^ mask) for d in range(ways)])]
    dynamic_slice x0 -> x1, local copies, waits for them, and re-layouts: none -> 2.7 us  [exchange_in_pairs(): lax.dynamic_slice_in_dim(shard, (here ^ mask) * width, width, axis=split)]
  transfers between devices with their start and end apart: 1 -> 16, of which waited for: 1 -> 11; matrix products, arithmetic and copies ran while one was open for 0% -> 0% of each run, Pallas kernels for 0% -> 0%
where the time goes in v1:
time: 196 us
  waiting for transfers between devices  124 us (63%)
  matrix products  40.5 us (21%)
  starting transfers between devices  24 us (12%)
  local copies, waits for them, and re-layouts  6.16 us (3%)
    all_to_all x1, waiting for transfers between devices, shards(): lax.all_to_all(partial_value, 'expert', split_axis=0, concat_axis=0, tile...  81.3 us
    ppermute x15, waiting for transfers between devices, exchange_in_pairs(): part = lax.ppermute(part, axis, [(d, d ^ mask) for d in range(ways)])  42.7 us
    dot_general x1, matrix products, shards(): result = jnp.dot(hidden, down_proj, preferred_element_type=jnp.float32)  21 us
    ppermute x15, starting transfers between devices, exchange_in_pairs(): part = lax.ppermute(part, axis, [(d, d ^ mask) for d in range(ways)])  17.7 us
    dot_general x1, matrix products, shards(): gate_val = jnp.dot(flat_rows, gate_proj, preferred_element_type=jnp.float32)  12.9 us
    all_to_all x1, starting transfers between devices, shards(): lax.all_to_all(partial_value, 'expert', split_axis=0, concat_axis=0, tile...  6.31 us
    dot_general x1, matrix products, shards(): jnp.einsum('tec,escd->td', combine_w, returned, precision=lax.Precision.H...  6.16 us
  transfers between devices with their start and end apart: 16, of which 11 were waited for; matrix products, arithmetic and copies ran while one was open for 0% of the time, Pallas kernels for 0%

profile of v1, /device:TPU:15, one launch (start us, length us, event | category | flops | bytes accessed | tf_op | source)
XLA Modules:
  0.0 196.0 jit_solution(5580824444786270734)
XLA Ops:
  0.0 0.0 copy-start
  0.0 0.8 convert_reduce_fusion
  0.8 0.0 copy-start.5
  0.9 0.0 copy-start.2
  1.0 0.0 copy-done
  1.0 0.5 convolution_convert_fusion
  1.5 2.7 %constant_dynamic-slice_fusion = (bf16[1,5,7168]{2,0,1:T(2,128)(2,1)S(1)}, bf16[1,5,7168]{2,0,1:T(2,128)(2,1)S(1)}, bf16[1,5,7168]{2,0,1:T(2,128)(2,1)S(1)}, bf1...) fusion(bf16[16,5,7168]{2,0,1:T(8,128)(2,1)S(1)} %convolution_co, ...), kind=kLoop, calls=%fused_computation.36 | loop fusion | bytes 2293824 | tf_op jit(solution)/shard_map/dynamic_slice | solution.py:20
  4.2 0.0 copy-done.5
  4.2 0.0 copy-done.2
  4.2 0.7 collective-permute-start
  4.9 0.3 collective-permute-start.1
  5.2 1.4 collective-permute-start.2
  6.7 0.2 collective-permute-start.3
  6.8 1.6 collective-permute-start.4
  8.5 0.2 broadcast_in_dim.38
  8.7 0.0 collective-permute-done
  8.7 0.2 collective-permute-start.5
  8.9 1.3 collective-permute-done.1
  10.3 1.3 collective-permute-start.6
  11.7 2.2 %collective-permute-done.2 = bf16[1,5,7168]{2,0,1:T(2,128)(2,1)S(1)} collective-permute-done((bf16[1,5,7168]{2,0,1:T(2,128)(2,1)S(1)}, bf16[1,5,7168]{2,0,1:T(2,128)(2,1)S(1)}, u32[]{:S(2)}, u32[]{:S(2)}) %collective-permute-start.2) | collective-permute-done | bytes 71712 | tf_op jit(solution)/shard_map/ppermute | solution.py:22
  13.8 2.3 %collective-permute-start.7 = (bf16[1,5,7168]{2,0,1:T(2,128)(2,1)S(1)}, bf16[1,5,7168]{2,0,1:T(2,128)(2,1)S(1)}, u32[]{:S(2)}, u32[]{:S(2)}) collective-permute-start(bf16[1,5,7168]{2,0,1:T(2,128)(2,1)S(1)} %get-tuple-element.12), channel_id=1, source_target_pairs={{0,8},{1,9},{2,10},{3,11},{4,12},{5,13},{6,14},{7,15},{8,0},{9,1},... | collective-permute-start | bytes 215048 | tf_op jit(solution)/shard_map/ppermute | solution.py:22
  16.2 0.0 collective-permute-done.3
  16.2 0.2 collective-permute-start.8
  16.4 0.0 collective-permute-done.4
  16.5 2.3 %collective-permute-start.9 = (bf16[1,5,7168]{2,0,1:T(2,128)(2,1)S(1)}, bf16[1,5,7168]{2,0,1:T(2,128)(2,1)S(1)}, u32[]{:S(2)}, u32[]{:S(2)}) collective-permute-start(bf16[1,5,7168]{2,0,1:T(2,128)(2,1)S(1)} %get-tuple-element.10), channel_id=1, source_target_pairs={{0,10},{1,11},{2,8},{3,9},{4,14},{5,15},{6,12},{7,13},{8,2},{9,3},... | collective-permute-start | bytes 215048 | tf_op jit(solution)/shard_map/ppermute | solution.py:22
  18.8 2.8 %collective-permute-done.5 = bf16[1,5,7168]{2,0,1:T(2,128)(2,1)S(1)} collective-permute-done((bf16[1,5,7168]{2,0,1:T(2,128)(2,1)S(1)}, bf16[1,5,7168]{2,0,1:T(2,128)(2,1)S(1)}, u32[]{:S(2)}, u32[]{:S(2)}) %collective-permute-start.5) | collective-permute-done | bytes 71712 | tf_op jit(solution)/shard_map/ppermute | solution.py:22
  21.7 5.0 %collective-permute-start.10 = (bf16[1,5,7168]{2,0,1:T(2,128)(2,1)S(1)}, bf16[1,5,7168]{2,0,1:T(2,128)(2,1)S(1)}, u32[]{:S(2)}, u32[]{:S(2)}) collective-permute-start(bf16[1,5,7168]{2,0,1:T(2,128)(2,1)S(1)} %get-tuple-element.9), channel_id=1, source_target_pairs={{0,11},{1,10},{2,9},{3,8},{4,15},{5,14},{6,13},{7,12},{8,3},{9,2},... | collective-permute-start | bytes 215048 | tf_op jit(solution)/shard_map/ppermute | solution.py:22
  26.7 0.0 collective-permute-done.6
  26.7 1.4 collective-permute-start.11
  28.2 0.0 collective-permute-done.7
  28.2 0.1 collective-permute-start.12
  28.3 12.6 %collective-permute-done.8 = bf16[1,5,7168]{2,0,1:T(2,128)(2,1)S(1)} collective-permute-done((bf16[1,5,7168]{2,0,1:T(2,128)(2,1)S(1)}, bf16[1,5,7168]{2,0,1:T(2,128)(2,1)S(1)}, u32[]{:S(2)}, u32[]{:S(2)}) %collective-permute-start.8) | collective-permute-done | bytes 71712 | tf_op jit(solution)/shard_map/ppermute | solution.py:22
  40.9 0.0 collective-permute-start.13
  41.0 3.0 %collective-permute-done.9 = bf16[1,5,7168]{2,0,1:T(2,128)(2,1)S(1)} collective-permute-done((bf16[1,5,7168]{2,0,1:T(2,128)(2,1)S(1)}, bf16[1,5,7168]{2,0,1:T(2,128)(2,1)S(1)}, u32[]{:S(2)}, u32[]{:S(2)}) %collective-permute-start.9) | collective-permute-done | bytes 71712 | tf_op jit(solution)/shard_map/ppermute | solution.py:22
  44.0 0.6 collective-permute-start.14
  44.6 5.5 %collective-permute-done.10 = bf16[1,5,7168]{2,0,1:T(2,128)(2,1)S(1)} collective-permute-done((bf16[1,5,7168]{2,0,1:T(2,128)(2,1)S(1)}, bf16[1,5,7168]{2,0,1:T(2,128)(2,1)S(1)}, u32[]{:S(2)}, u32[]{:S(2)}) %collective-permute-start.10) | collective-permute-done | bytes 71712 | tf_op jit(solution)/shard_map/ppermute | solution.py:22
  50.2 6.1 %collective-permute-done.11 = bf16[1,5,7168]{2,0,1:T(2,128)(2,1)S(1)} collective-permute-done((bf16[1,5,7168]{2,0,1:T(2,128)(2,1)S(1)}, bf16[1,5,7168]{2,0,1:T(2,128)(2,1)S(1)}, u32[]{:S(2)}, u32[]{:S(2)}) %collective-permute-start.11) | collective-permute-done | bytes 71712 | tf_op jit(solution)/shard_map/ppermute | solution.py:22
  56.3 3.4 %collective-permute-done.12 = bf16[1,5,7168]{2,0,1:T(2,128)(2,1)S(1)} collective-permute-done((bf16[1,5,7168]{2,0,1:T(2,128)(2,1)S(1)}, bf16[1,5,7168]{2,0,1:T(2,128)(2,1)S(1)}, u32[]{:S(2)}, u32[]{:S(2)}) %collective-permute-start.12) | collective-permute-done | bytes 71712 | tf_op jit(solution)/shard_map/ppermute | solution.py:22
  59.8 2.6 %collective-permute-done.13 = bf16[1,5,7168]{2,0,1:T(2,128)(2,1)S(1)} collective-permute-done((bf16[1,5,7168]{2,0,1:T(2,128)(2,1)S(1)}, bf16[1,5,7168]{2,0,1:T(2,128)(2,1)S(1)}, u32[]{:S(2)}, u32[]{:S(2)}) %collective-permute-start.13) | collective-permute-done | bytes 71712 | tf_op jit(solution)/shard_map/ppermute | solution.py:22
  62.5 3.0 %collective-permute-done.14 = bf16[1,5,7168]{2,0,1:T(2,128)(2,1)S(1)} collective-permute-done((bf16[1,5,7168]{2,0,1:T(2,128)(2,1)S(1)}, bf16[1,5,7168]{2,0,1:T(2,128)(2,1)S(1)}, u32[]{:S(2)}, u32[]{:S(2)}) %collective-permute-start.14) | collective-permute-done | bytes 71712 | tf_op jit(solution)/shard_map/ppermute | solution.py:22
  65.6 0.6 reshape.23
  66.1 12.9 %fusion.19 = f32[80,2048]{1,0:T(8,128)} fusion(bf16[80,7168]{1,0:T(8,128)(2,1)S(1)} %reshape.23, bf16[7168,2048]{1,0:T(8,128)(2,1)} %param.9), kind=kOutput, calls=%fused_computation.57 | convolution fusion | flops 2348810240 | bytes 31162368 | tf_op jit(solution)/shard_map/dot_general | solution.py:49
  79.0 21.0 %fusion.2 = f32[80,7168]{1,0:T(8,128)S(1)} fusion(bf16[2048,7168]{1,0:T(8,128)(2,1)} %param.11, f32[80,2048]{1,0:T(8,128)} %fusion.19, bf16[80,7168]{1,0:T(8,128)(2,1)S(1)} %reshape.23, bf16[7168,2048]{1,0:T(8,128)(2,1)} %param.10), kind=kOutput, calls=%fused_computation.5 | convolution fusion | flops 4698603520 | bytes 62816256 | tf_op jit(solution)/shard_map/dot_general | solution.py:52
  100.0 2.1 %reshape.24 = f32[16,5,7168]{2,1,0:T(8,128)} reshape(f32[80,7168]{1,0:T(8,128)S(1)} %fusion.2) | data formatting | bytes 4587520 | tf_op jit(solution)/shard_map/reshape | solution.py:53
  102.1 0.0 copy-start.4
  102.1 0.0 copy-start.7
  102.1 0.0 copy-start.3
  102.1 0.0 copy-start.6
  102.1 6.3 %all-to-all-start = ((f32[16,5,7168]{2,1,0:T(8,128)}), f32[16,5,7168]{2,1,0:T(8,128)}, u32[]{:S(2)}, u32[]{:S(2)}) async-start(f32[16,5,7168]{2,1,0:T(8,128)} %reshape.24), calls=%async_computation | async-start | bytes 7340032 | tf_op jit(solution)/shard_map/all_to_all | solution.py:54
  108.4 0.0 copy-done.4
  108.4 0.0 copy-done.7
  108.4 0.0 copy-start.1
  108.4 0.1 select_reduce_fusion
  108.5 81.3 %all-to-all-done = f32[16,5,7168]{2,1,0:T(8,128)} async-done(((f32[16,5,7168]{2,1,0:T(8,128)}), f32[16,5,7168]{2,1,0:T(8,128)}, u32[]{:S(2)}, u32[]{:S(2)}) %all-to-all-start) | async-done | bytes 2293792 | tf_op jit(solution)/shard_map/all_to_all | solution.py:54
  189.9 0.0 copy-done.3
  189.9 0.0 copy-done.6
  189.9 6.2 %fusion = bf16[8,7168]{1,0:T(8,128)(2,1)} fusion(f32[16,5,7168]{2,1,0:T(8,128)} %all-to-all-done, f32[8,16]{1,0:T(8,128)S(1)} %select_reduce_fusion, s32[8,16]{1,0:T(8,128)S(1)} %copy-done.3, pred[8,16]{1,0:T(8,128)(4,1)S(1)} %copy-done.6), kind=kOutput, calls=%fused_computation.2 | convolution fusion | flops 55109504 | bytes 2409600 | tf_op jit(solution)/shard_map/tec,escd->td/dot_general | solution.py:56
  196.0 0.0 copy-done.1
  (19 shorter events, 0.7 us)
Async XLA Ops:
  0.0 1.0 copy-start
  0.8 3.3 %copy-start.5 = (pred[8,16]{1,0:T(8,128)(4,1)}, pred[8,16]{1,0:T(8,128)(4,1)S(1)}, u32[]{:S(2)}) copy-start(pred[8,16]{1,0:T(8,128)(4,1)S(1)} %broadcast_compare_fusion) | copy-start | bytes 388
  0.9 3.3 %copy-start.2 = (s32[8,16]{1,0:T(8,128)}, s32[8,16]{1,0:T(8,128)S(1)}, u32[]{:S(2)}) copy-start(s32[8,16]{1,0:T(8,128)S(1)} %broadcast_add_fusion) | copy-start | bytes 1540
  4.2 4.5 %collective-permute-start = (bf16[1,5,7168]{2,0,1:T(2,128)(2,1)S(1)}, bf16[1,5,7168]{2,0,1:T(2,128)(2,1)S(1)}, u32[]{:S(2)}, u32[]{:S(2)}) collective-permute-start(bf16[1,5,7168]{2,0,1:T(2,128)(2,1)S(1)} %get-tuple-element.19), channel_id=1, source_target_pairs={{0,1},{1,0},{2,3},{3,2},{4,5},{5,4},{6,7},{7,6},{8,9},{9,8},{10,11... | collective-permute-start | bytes 215048 | tf_op jit(solution)/shard_map/ppermute | solution.py:22
  4.9 5.3 %collective-permute-start.1 = (bf16[1,5,7168]{2,0,1:T(2,128)(2,1)S(1)}, bf16[1,5,7168]{2,0,1:T(2,128)(2,1)S(1)}, u32[]{:S(2)}, u32[]{:S(2)}) collective-permute-start(bf16[1,5,7168]{2,0,1:T(2,128)(2,1)S(1)} %get-tuple-element.18), channel_id=1, source_target_pairs={{0,2},{1,3},{2,0},{3,1},{4,6},{5,7},{6,4},{7,5},{8,10},{9,11},{10,... | collective-permute-start | bytes 215048 | tf_op jit(solution)/shard_map/ppermute | solution.py:22
  5.2 8.6 %collective-permute-start.2 = (bf16[1,5,7168]{2,0,1:T(2,128)(2,1)S(1)}, bf16[1,5,7168]{2,0,1:T(2,128)(2,1)S(1)}, u32[]{:S(2)}, u32[]{:S(2)}) collective-permute-start(bf16[1,5,7168]{2,0,1:T(2,128)(2,1)S(1)} %get-tuple-element.17), channel_id=1, source_target_pairs={{0,3},{1,2},{2,1},{3,0},{4,7},{5,6},{6,5},{7,4},{8,11},{9,10},{10,... | collective-permute-start | bytes 215048 | tf_op jit(solution)/shard_map/ppermute | solution.py:22
  6.7 9.5 %collective-permute-start.3 = (bf16[1,5,7168]{2,0,1:T(2,128)(2,1)S(1)}, bf16[1,5,7168]{2,0,1:T(2,128)(2,1)S(1)}, u32[]{:S(2)}, u32[]{:S(2)}) collective-permute-start(bf16[1,5,7168]{2,0,1:T(2,128)(2,1)S(1)} %get-tuple-element.16), channel_id=1, source_target_pairs={{0,4},{1,5},{2,6},{3,7},{4,0},{5,1},{6,2},{7,3},{8,12},{9,13},{10,... | collective-permute-start | bytes 215048 | tf_op jit(solution)/shard_map/ppermute | solution.py:22
  6.8 9.6 %collective-permute-start.4 = (bf16[1,5,7168]{2,0,1:T(2,128)(2,1)S(1)}, bf16[1,5,7168]{2,0,1:T(2,128)(2,1)S(1)}, u32[]{:S(2)}, u32[]{:S(2)}) collective-permute-start(bf16[1,5,7168]{2,0,1:T(2,128)(2,1)S(1)} %get-tuple-element.15), channel_id=1, source_target_pairs={{0,5},{1,4},{2,7},{3,6},{4,1},{5,0},{6,3},{7,2},{8,13},{9,12},{10,... | collective-permute-start | bytes 215048 | tf_op jit(solution)/shard_map/ppermute | solution.py:22
  8.7 13.0 %collective-permute-start.5 = (bf16[1,5,7168]{2,0,1:T(2,128)(2,1)S(1)}, bf16[1,5,7168]{2,0,1:T(2,128)(2,1)S(1)}, u32[]{:S(2)}, u32[]{:S(2)}) collective-permute-start(bf16[1,5,7168]{2,0,1:T(2,128)(2,1)S(1)} %get-tuple-element.14), channel_id=1, source_target_pairs={{0,6},{1,7},{2,4},{3,5},{4,2},{5,3},{6,0},{7,1},{8,14},{9,15},{10,... | collective-permute-start | bytes 215048 | tf_op jit(solution)/shard_map/ppermute | solution.py:22
  10.3 16.5 %collective-permute-start.6 = (bf16[1,5,7168]{2,0,1:T(2,128)(2,1)S(1)}, bf16[1,5,7168]{2,0,1:T(2,128)(2,1)S(1)}, u32[]{:S(2)}, u32[]{:S(2)}) collective-permute-start(bf16[1,5,7168]{2,0,1:T(2,128)(2,1)S(1)} %get-tuple-element.13), channel_id=1, source_target_pairs={{0,7},{1,6},{2,5},{3,4},{4,3},{5,2},{6,1},{7,0},{8,15},{9,14},{10,... | collective-permute-start | bytes 215048 | tf_op jit(solution)/shard_map/ppermute | solution.py:22
  13.8 14.4 %collective-permute-start.7 = (bf16[1,5,7168]{2,0,1:T(2,128)(2,1)S(1)}, bf16[1,5,7168]{2,0,1:T(2,128)(2,1)S(1)}, u32[]{:S(2)}, u32[]{:S(2)}) collective-permute-start(bf16[1,5,7168]{2,0,1:T(2,128)(2,1)S(1)} %get-tuple-element.12), channel_id=1, source_target_pairs={{0,8},{1,9},{2,10},{3,11},{4,12},{5,13},{6,14},{7,15},{8,0},{9,1},... | collective-permute-start | bytes 215048 | tf_op jit(solution)/shard_map/ppermute | solution.py:22
  16.2 24.8 %collective-permute-start.8 = (bf16[1,5,7168]{2,0,1:T(2,128)(2,1)S(1)}, bf16[1,5,7168]{2,0,1:T(2,128)(2,1)S(1)}, u32[]{:S(2)}, u32[]{:S(2)}) collective-permute-start(bf16[1,5,7168]{2,0,1:T(2,128)(2,1)S(1)} %get-tuple-element.11), channel_id=1, source_target_pairs={{0,9},{1,8},{2,11},{3,10},{4,13},{5,12},{6,15},{7,14},{8,1},{9,0},... | collective-permute-start | bytes 215048 | tf_op jit(solution)/shard_map/ppermute | solution.py:22
  16.5 27.6 %collective-permute-start.9 = (bf16[1,5,7168]{2,0,1:T(2,128)(2,1)S(1)}, bf16[1,5,7168]{2,0,1:T(2,128)(2,1)S(1)}, u32[]{:S(2)}, u32[]{:S(2)}) collective-permute-start(bf16[1,5,7168]{2,0,1:T(2,128)(2,1)S(1)} %get-tuple-element.10), channel_id=1, source_target_pairs={{0,10},{1,11},{2,8},{3,9},{4,14},{5,15},{6,12},{7,13},{8,2},{9,3},... | collective-permute-start | bytes 215048 | tf_op jit(solution)/shard_map/ppermute | solution.py:22
  21.7 28.5 %collective-permute-start.10 = (bf16[1,5,7168]{2,0,1:T(2,128)(2,1)S(1)}, bf16[1,5,7168]{2,0,1:T(2,128)(2,1)S(1)}, u32[]{:S(2)}, u32[]{:S(2)}) collective-permute-start(bf16[1,5,7168]{2,0,1:T(2,128)(2,1)S(1)} %get-tuple-element.9), channel_id=1, source_target_pairs={{0,11},{1,10},{2,9},{3,8},{4,15},{5,14},{6,13},{7,12},{8,3},{9,2},... | collective-permute-start | bytes 215048 | tf_op jit(solution)/shard_map/ppermute | solution.py:22
  26.7 29.6 %collective-permute-start.11 = (bf16[1,5,7168]{2,0,1:T(2,128)(2,1)S(1)}, bf16[1,5,7168]{2,0,1:T(2,128)(2,1)S(1)}, u32[]{:S(2)}, u32[]{:S(2)}) collective-permute-start(bf16[1,5,7168]{2,0,1:T(2,128)(2,1)S(1)} %get-tuple-element.8), channel_id=1, source_target_pairs={{0,12},{1,13},{2,14},{3,15},{4,8},{5,9},{6,10},{7,11},{8,4},{9,5},... | collective-permute-start | bytes 215048 | tf_op jit(solution)/shard_map/ppermute | solution.py:22
  28.2 31.6 %collective-permute-start.12 = (bf16[1,5,7168]{2,0,1:T(2,128)(2,1)S(1)}, bf16[1,5,7168]{2,0,1:T(2,128)(2,1)S(1)}, u32[]{:S(2)}, u32[]{:S(2)}) collective-permute-start(bf16[1,5,7168]{2,0,1:T(2,128)(2,1)S(1)} %get-tuple-element.7), channel_id=1, source_target_pairs={{0,13},{1,12},{2,15},{3,14},{4,9},{5,8},{6,11},{7,10},{8,5},{9,4},... | collective-permute-start | bytes 215048 | tf_op jit(solution)/shard_map/ppermute | solution.py:22
  40.9 21.5 %collective-permute-start.13 = (bf16[1,5,7168]{2,0,1:T(2,128)(2,1)S(1)}, bf16[1,5,7168]{2,0,1:T(2,128)(2,1)S(1)}, u32[]{:S(2)}, u32[]{:S(2)}) collective-permute-start(bf16[1,5,7168]{2,0,1:T(2,128)(2,1)S(1)} %get-tuple-element.6), channel_id=1, source_target_pairs={{0,14},{1,15},{2,12},{3,13},{4,10},{5,11},{6,8},{7,9},{8,6},{9,7},... | collective-permute-start | bytes 215048 | tf_op jit(solution)/shard_map/ppermute | solution.py:22
  44.0 21.5 %collective-permute-start.14 = (bf16[1,5,7168]{2,0,1:T(2,128)(2,1)S(1)}, bf16[1,5,7168]{2,0,1:T(2,128)(2,1)S(1)}, u32[]{:S(2)}, u32[]{:S(2)}) collective-permute-start(bf16[1,5,7168]{2,0,1:T(2,128)(2,1)S(1)} %get-tuple-element.5), channel_id=1, source_target_pairs={{0,15},{1,14},{2,13},{3,12},{4,11},{5,10},{6,9},{7,8},{8,7},{9,6},... | collective-permute-start | bytes 215048 | tf_op jit(solution)/shard_map/ppermute | solution.py:22
  102.1 6.3 %copy-start.4 = (s32[8,8]{1,0:T(8,128)S(1)}, s32[8,8]{1,0:T(8,128)}, u32[]{:S(2)}) copy-start(s32[8,8]{1,0:T(8,128)} %param.7) | copy-start | bytes 772
  102.1 6.3 %copy-start.7 = (f32[8,8]{1,0:T(8,128)S(1)}, f32[8,8]{1,0:T(8,128)}, u32[]{:S(2)}) copy-start(f32[8,8]{1,0:T(8,128)} %param.8) | copy-start | bytes 772
  102.1 87.8 %copy-start.3 = (s32[8,16]{1,0:T(8,128)S(1)}, s32[8,16]{1,0:T(8,128)}, u32[]{:S(2)}) copy-start(s32[8,16]{1,0:T(8,128)} %copy-done.2) | copy-start | bytes 1540
  102.1 87.8 %copy-start.6 = (pred[8,16]{1,0:T(8,128)(4,1)S(1)}, pred[8,16]{1,0:T(8,128)(4,1)}, u32[]{:S(2)}) copy-start(pred[8,16]{1,0:T(8,128)(4,1)} %copy-done.5) | copy-start | bytes 388
  102.1 87.8 %all-to-all-start = ((f32[16,5,7168]{2,1,0:T(8,128)}), f32[16,5,7168]{2,1,0:T(8,128)}, u32[]{:S(2)}, u32[]{:S(2)}) async-start(f32[16,5,7168]{2,1,0:T(8,128)} %reshape.24), calls=%async_computation | async-start | bytes 7340032 | tf_op jit(solution)/shard_map/all_to_all | solution.py:54
  108.4 87.6 %copy-start.1 = (bf16[8,7168]{1,0:T(8,128)(2,1)S(1)}, bf16[8,7168]{1,0:T(8,128)(2,1)}, u32[]{:S(2)}) copy-start(bf16[8,7168]{1,0:T(8,128)(2,1)} %param.6) | copy-start | bytes 344068
